TPU v7x, 256 devices: a whole 4x4x8 slice. The times are simulated.
256 devices in a mesh: seq: 32 (over y, x, z_hi), head: 8 (over z_lo, core).
Axes of the slice: x: 4, y: 4, z: 8 (z_hi: 2, z_lo: 4; z = z_hi * 4 + z_lo), core: 2. Of those that a mesh axis runs over, the one named last changes fastest.
Arguments:
- queries: bfloat16 [16384, 4096], P(('seq', 'head')), may hold values from -72 to 72
- keys: bfloat16 [16384, 2048], P(('seq', 'head')), may hold values from -6 to 6
- values: bfloat16 [16384, 2048], P(('seq', 'head')), may hold values from -6 to 6
- prefix_keys: bfloat16 [4096, 2048], P(None, 'head'), may hold values from -10 to 10
- prefix_values: bfloat16 [4096, 2048], P(None, 'head'), may hold values from -6 to 6
- span_start: int32 [1], replicated, may hold values from 0 to 4095
Outputs:
- attended: bfloat16 [16384, 4096], P(('seq', 'head'))
All inputs are finite; a program needn't handle non-finite values.
Results may differ from a plain program's by a relative error of at most 0.003.
Values may be sent and summed in bfloat16 or wider, within the bound.
A program may use at most 128 MiB of HBM per device.

v0:
```python
import jax
import jax.numpy as jnp
from jax import lax
from jax.sharding import PartitionSpec as P

HEAD_DIM = 128
QH = 32
KVH = 16
QSCALE = 144
WINDOW = 4096


def shifted(shard, axis, by):
    size = lax.axis_size(axis)
    pairs = [(i, i + by) for i in range(size) if 0 <= i + by < size]
    return lax.ppermute(shard, axis, pairs)


def shortened(shard):
    return jax.tree.map(lambda a: a.astype(jnp.bfloat16) if a.dtype == jnp.float32 else a, shard)


def attend_block(query_rows, key_rows, value_rows, query_first, key_first, start_value):
    block_rows = query_rows.shape[0]
    key_count = key_rows.shape[0]
    grouping = QH // KVH
    scaling = QSCALE ** (-0.5)
    local_groups = key_rows.shape[1] // HEAD_DIM
    query_pos = query_first + jnp.arange(block_rows, dtype=jnp.int32)
    key_pos = key_first + jnp.arange(key_count, dtype=jnp.int32)
    distance = query_pos[:, None] - key_pos[None, :]
    allowed = (distance >= 0) & (distance < WINDOW) & (start_value + key_pos >= 0)[None, :]
    outputs = []
    for key_group in range(local_groups):
        lower = key_group * grouping * HEAD_DIM
        query_head = query_rows[:, lower : lower + grouping * HEAD_DIM].reshape(
            block_rows, grouping, HEAD_DIM
        )
        key_head = key_rows[:, key_group * HEAD_DIM : (key_group + 1) * HEAD_DIM]
        value_head = value_rows[:, key_group * HEAD_DIM : (key_group + 1) * HEAD_DIM]
        scores = (
            jnp.einsum("qgd,kd->gqk", query_head, key_head, preferred_element_type=jnp.float32)
            * scaling
        )
        scores = jnp.where(allowed[None], scores, -jnp.inf)
        peak_score = jnp.max(scores, axis=2, keepdims=True)
        unnormed = jnp.exp(scores - peak_score)
        totals = jnp.sum(unnormed, axis=2)
        weights = unnormed.astype(jnp.bfloat16)
        mixture = jnp.einsum("gqk,kd->qgd", weights, value_head, preferred_element_type=jnp.float32)
        outputs.append(
            (mixture / jnp.transpose(totals)[:, :, None]).reshape(block_rows, grouping * HEAD_DIM)
        )
    return jnp.concatenate(outputs, axis=1).astype(jnp.bfloat16)


def shards(queries, keys, values, prefix_keys, prefix_values, span_start):
    query_local, key_local, value_local = (
        lax.all_to_all(queries, "head", split_axis=1, concat_axis=0, tiled=True),
        lax.all_to_all(keys, "head", split_axis=1, concat_axis=0, tiled=True),
        lax.all_to_all(values, "head", split_axis=1, concat_axis=0, tiled=True),
    )
    seq_rows = query_local.shape[0]
    shards_back = WINDOW // seq_rows
    seq_index = lax.axis_index("seq")

    def relay(step, carried):
        moving_keys, moving_values, window_keys, window_values = carried
        moving_keys, moving_values = shifted((moving_keys, moving_values), "seq", 1)
        offset = (shards_back - 1 - step) * seq_rows
        window_keys = lax.dynamic_update_slice_in_dim(window_keys, moving_keys, offset, 0)
        window_values = lax.dynamic_update_slice_in_dim(window_values, moving_values, offset, 0)
        return (moving_keys, moving_values, window_keys, window_values)

    empty = jnp.zeros((WINDOW, key_local.shape[1]), jnp.bfloat16)
    carried = lax.fori_loop(0, shards_back, relay, (key_local, value_local, empty, empty))
    window_keys = carried[2]
    window_values = carried[3]
    first_row = jnp.minimum(seq_index * seq_rows, WINDOW)
    padded_keys = jnp.concatenate([prefix_keys, jnp.zeros_like(prefix_keys)], axis=0)
    padded_values = jnp.concatenate([prefix_values, jnp.zeros_like(prefix_values)], axis=0)
    window_keys = window_keys + lax.dynamic_slice_in_dim(padded_keys, first_row, WINDOW, 0)
    window_values = window_values + lax.dynamic_slice_in_dim(padded_values, first_row, WINDOW, 0)
    all_keys = jnp.concatenate([window_keys, key_local], axis=0)
    all_values = jnp.concatenate([window_values, value_local], axis=0)
    block_rows = min(512, seq_rows)
    block_count = seq_rows // block_rows
    start_value = span_start[0]
    key_base = (seq_index - shards_back) * seq_rows
    query_base = seq_index * seq_rows

    def one_block(block_index):
        first = block_index * block_rows
        return attend_block(
            query_local, all_keys, all_values, query_base + first, key_base + first, start_value
        )

    blocks = lax.map(one_block, jnp.arange(block_count, dtype=jnp.int32))
    attended = blocks.reshape(seq_rows, query_local.shape[1])
    return lax.all_to_all(
        shortened(attended), "head", split_axis=0, concat_axis=1, tiled=True
    ).astype(attended.dtype)


def solution(mesh):
    placed = (
        P(("seq", "head"), None),
        P(("seq", "head"), None),
        P(("seq", "head"), None),
        P(None, "head"),
        P(None, "head"),
        P(),
    )
    return jax.shard_map(
        shards, mesh=mesh, in_specs=placed, out_specs=P(("seq", "head"), None), check_vma=False
    )
```

profile of v0, /device:TPU:16, one launch (start us, length us, event | category | flops | bytes accessed | tf_op | source)
XLA Modules:
  0.0 381.9 jit_solution(13669239722404619152)
XLA Ops:
  0.0 1.7 copy.73
  1.7 5.9 %all-to-all-start.1 = ((bf16[64,8,256]{2,0,1:T(8,128)(2,1)}), bf16[64,8,256]{2,0,1:T(8,128)(2,1)}, u32[]{:S(2)}, u32[]{:S(2)}) async-start(bf16[64,8,256]{2,0,1:T(8,128)(2,1)} %bitcast.95), calls=%async_computation.1 | async-start | bytes 524288 | tf_op jit(solution)/shard_map/all_to_all | solution.py:61
  8.3 1.7 copy.74
  10.0 7.5 %all-to-all-done.1 = bf16[64,8,256]{2,0,1:T(8,128)(2,1)} async-done(((bf16[64,8,256]{2,0,1:T(8,128)(2,1)}), bf16[64,8,256]{2,0,1:T(8,128)(2,1)}, u32[]{:S(2)}, u32[]{:S(2)}) %all-to-all-start.1) | async-done | bytes 262176 | tf_op jit(solution)/shard_map/all_to_all | solution.py:61
  17.5 3.4 all-to-all-start
  20.9 3.8 %fusion.11 = pred[512,4608]{0,1:T(8,128)(4,1)S(1)} fusion(s32[4608]{0:T(1024)S(1)} %iota_add_fusion, s32[512]{0:T(512)S(1)} %iota_add_fusion.1, pred[4608]{0:T(1024)(128)(4,1)S(1)} %add_compare_fusion), kind=kLoop, calls=%fused_computation.17 | loop fusion | flops 11796480 | bytes 2384384 | tf_op jit(solution)/shard_map/while/body/eval_jaxpr/and | solution.py:32
  24.8 0.8 copy.72
  25.6 4.1 %copy.44 = bf16[4096,256]{0,1:T(8,128)(2,1)} copy(bf16[4096,256]{1,0:T(8,128)(2,1)} %param.12) | data formatting | bytes 4194304 | tf_op args[4]
  29.7 1.8 copy.46
  31.5 5.0 %all-to-all-start.2 = ((bf16[64,8,512]{2,0,1:T(8,128)(2,1)}), bf16[64,8,512]{2,0,1:T(8,128)(2,1)}, u32[]{:S(2)}, u32[]{:S(2)}) async-start(bf16[64,8,512]{2,0,1:T(8,128)(2,1)} %bitcast.94), calls=%async_computation.2 | async-start | bytes 1048576 | tf_op jit(solution)/shard_map/all_to_all | solution.py:59
  37.3 1.6 broadcast.86.clone
  38.8 1.4 broadcast.86
  40.3 204.3 %while.6 = (s32[]{:T(128)}, bf16[512,256]{1,0:T(8,128)(2,1)}, bf16[512,256]{1,0:T(8,128)(2,1)}, bf16[4096,256]{1,0:T(8,128)(2,1)}, bf16[4096,256]{0,1:T(8,128)(2...) while((s32[]{:T(128)}, bf16[512,256]{1,0:T(8,128)(2,1)}, bf16[512,256]{1,0:T(8,128)(2,1)}, ...), condition=%wide.region_1.0_spmd, body=%wide.region_0.0_spmd.sunk | while | flops 7 | bytes 4718839 | solution.py:76
  40.3 7.1 %collective-permute-start.1 = (bf16[512,256]{1,0:T(8,128)(2,1)}, bf16[512,256]{1,0:T(8,128)(2,1)S(1)}, u32[]{:S(2)}, u32[]{:S(2)}) collective-permute-start(bf16[512,256]{1,0:T(8,128)(2,1)} %get-tuple-element.191), channel_id=1, source_target_pairs={{0,8},{8,16},{16,24},{24,32},{32,40},{40,48},{48,56},{56,64},{64,7... | collective-permute-start | bytes 786440 | tf_op jit(solution)/shard_map/while/body/eval_jaxpr/ppermute | solution.py:16
  47.4 3.5 collective-permute-start
  51.0 10.3 %collective-permute-done.1 = bf16[512,256]{1,0:T(8,128)(2,1)S(1)} collective-permute-done((bf16[512,256]{1,0:T(8,128)(2,1)}, bf16[512,256]{1,0:T(8,128)(2,1)S(1)}, u32[]{:S(2)}, u32[]{:S(2)}) %collective-permute-start.1) | collective-permute-done | bytes 262176 | tf_op jit(solution)/shard_map/while/body/eval_jaxpr/ppermute | solution.py:16
  62.1 0.7 constant_dynamic-update-slice_fusion.5
  62.8 6.7 %collective-permute-done = bf16[512,256]{1,0:T(8,128)(2,1)S(1)} collective-permute-done((bf16[512,256]{1,0:T(8,128)(2,1)}, bf16[512,256]{1,0:T(8,128)(2,1)S(1)}, u32[]{:S(2)}, u32[]{:S(2)}) %collective-permute-start) | collective-permute-done | bytes 262176 | tf_op jit(solution)/shard_map/while/body/eval_jaxpr/ppermute | solution.py:16
  71.0 2.6 collective-permute-start.1
  73.6 5.9 %collective-permute-start = (bf16[512,256]{1,0:T(8,128)(2,1)}, bf16[512,256]{1,0:T(8,128)(2,1)S(1)}, u32[]{:S(2)}, u32[]{:S(2)}) collective-permute-start(bf16[512,256]{1,0:T(8,128)(2,1)} %get-tuple-element.190), channel_id=1, source_target_pairs={{0,8},{8,16},{16,24},{24,32},{32,40},{40,48},{48,56},{56,64},{64,7... | collective-permute-start | bytes 786440 | tf_op jit(solution)/shard_map/while/body/eval_jaxpr/ppermute | solution.py:16
  79.6 9.6 %collective-permute-done.1 = bf16[512,256]{1,0:T(8,128)(2,1)S(1)} collective-permute-done((bf16[512,256]{1,0:T(8,128)(2,1)}, bf16[512,256]{1,0:T(8,128)(2,1)S(1)}, u32[]{:S(2)}, u32[]{:S(2)}) %collective-permute-start.1) | collective-permute-done | bytes 262176 | tf_op jit(solution)/shard_map/while/body/eval_jaxpr/ppermute | solution.py:16
  90.0 0.8 constant_dynamic-update-slice_fusion.5
  90.8 3.2 collective-permute-done
  95.5 1.9 collective-permute-start.1
  97.4 4.3 %collective-permute-start = (bf16[512,256]{1,0:T(8,128)(2,1)}, bf16[512,256]{1,0:T(8,128)(2,1)S(1)}, u32[]{:S(2)}, u32[]{:S(2)}) collective-permute-start(bf16[512,256]{1,0:T(8,128)(2,1)} %get-tuple-element.190), channel_id=1, source_target_pairs={{0,8},{8,16},{16,24},{24,32},{32,40},{40,48},{48,56},{56,64},{64,7... | collective-permute-start | bytes 786440 | tf_op jit(solution)/shard_map/while/body/eval_jaxpr/ppermute | solution.py:16
  101.7 12.0 %collective-permute-done.1 = bf16[512,256]{1,0:T(8,128)(2,1)S(1)} collective-permute-done((bf16[512,256]{1,0:T(8,128)(2,1)}, bf16[512,256]{1,0:T(8,128)(2,1)S(1)}, u32[]{:S(2)}, u32[]{:S(2)}) %collective-permute-start.1) | collective-permute-done | bytes 262176 | tf_op jit(solution)/shard_map/while/body/eval_jaxpr/ppermute | solution.py:16
  114.6 0.8 constant_dynamic-update-slice_fusion.5
  115.3 2.3 collective-permute-done
  119.0 1.9 collective-permute-start.1
  120.9 4.8 %collective-permute-start = (bf16[512,256]{1,0:T(8,128)(2,1)}, bf16[512,256]{1,0:T(8,128)(2,1)S(1)}, u32[]{:S(2)}, u32[]{:S(2)}) collective-permute-start(bf16[512,256]{1,0:T(8,128)(2,1)} %get-tuple-element.190), channel_id=1, source_target_pairs={{0,8},{8,16},{16,24},{24,32},{32,40},{40,48},{48,56},{56,64},{64,7... | collective-permute-start | bytes 786440 | tf_op jit(solution)/shard_map/while/body/eval_jaxpr/ppermute | solution.py:16
  125.8 12.2 %collective-permute-done.1 = bf16[512,256]{1,0:T(8,128)(2,1)S(1)} collective-permute-done((bf16[512,256]{1,0:T(8,128)(2,1)}, bf16[512,256]{1,0:T(8,128)(2,1)S(1)}, u32[]{:S(2)}, u32[]{:S(2)}) %collective-permute-start.1) | collective-permute-done | bytes 262176 | tf_op jit(solution)/shard_map/while/body/eval_jaxpr/ppermute | solution.py:16
  138.9 0.8 constant_dynamic-update-slice_fusion.5
  139.6 4.0 %collective-permute-done = bf16[512,256]{1,0:T(8,128)(2,1)S(1)} collective-permute-done((bf16[512,256]{1,0:T(8,128)(2,1)}, bf16[512,256]{1,0:T(8,128)(2,1)S(1)}, u32[]{:S(2)}, u32[]{:S(2)}) %collective-permute-start) | collective-permute-done | bytes 262176 | tf_op jit(solution)/shard_map/while/body/eval_jaxpr/ppermute | solution.py:16
  145.1 1.9 collective-permute-start.1
  147.0 4.5 %collective-permute-start = (bf16[512,256]{1,0:T(8,128)(2,1)}, bf16[512,256]{1,0:T(8,128)(2,1)S(1)}, u32[]{:S(2)}, u32[]{:S(2)}) collective-permute-start(bf16[512,256]{1,0:T(8,128)(2,1)} %get-tuple-element.190), channel_id=1, source_target_pairs={{0,8},{8,16},{16,24},{24,32},{32,40},{40,48},{48,56},{56,64},{64,7... | collective-permute-start | bytes 786440 | tf_op jit(solution)/shard_map/while/body/eval_jaxpr/ppermute | solution.py:16
  151.5 11.7 %collective-permute-done.1 = bf16[512,256]{1,0:T(8,128)(2,1)S(1)} collective-permute-done((bf16[512,256]{1,0:T(8,128)(2,1)}, bf16[512,256]{1,0:T(8,128)(2,1)S(1)}, u32[]{:S(2)}, u32[]{:S(2)}) %collective-permute-start.1) | collective-permute-done | bytes 262176 | tf_op jit(solution)/shard_map/while/body/eval_jaxpr/ppermute | solution.py:16
  164.1 0.8 constant_dynamic-update-slice_fusion.5
  164.8 3.2 collective-permute-done
  169.5 1.9 collective-permute-start.1
  171.4 4.1 %collective-permute-start = (bf16[512,256]{1,0:T(8,128)(2,1)}, bf16[512,256]{1,0:T(8,128)(2,1)S(1)}, u32[]{:S(2)}, u32[]{:S(2)}) collective-permute-start(bf16[512,256]{1,0:T(8,128)(2,1)} %get-tuple-element.190), channel_id=1, source_target_pairs={{0,8},{8,16},{16,24},{24,32},{32,40},{40,48},{48,56},{56,64},{64,7... | collective-permute-start | bytes 786440 | tf_op jit(solution)/shard_map/while/body/eval_jaxpr/ppermute | solution.py:16
  175.5 12.2 %collective-permute-done.1 = bf16[512,256]{1,0:T(8,128)(2,1)S(1)} collective-permute-done((bf16[512,256]{1,0:T(8,128)(2,1)}, bf16[512,256]{1,0:T(8,128)(2,1)S(1)}, u32[]{:S(2)}, u32[]{:S(2)}) %collective-permute-start.1) | collective-permute-done | bytes 262176 | tf_op jit(solution)/shard_map/while/body/eval_jaxpr/ppermute | solution.py:16
  188.6 0.8 constant_dynamic-update-slice_fusion.5
  189.4 4.0 %collective-permute-done = bf16[512,256]{1,0:T(8,128)(2,1)S(1)} collective-permute-done((bf16[512,256]{1,0:T(8,128)(2,1)}, bf16[512,256]{1,0:T(8,128)(2,1)S(1)}, u32[]{:S(2)}, u32[]{:S(2)}) %collective-permute-start) | collective-permute-done | bytes 262176 | tf_op jit(solution)/shard_map/while/body/eval_jaxpr/ppermute | solution.py:16
  194.8 1.9 collective-permute-start.1
  196.7 4.5 %collective-permute-start = (bf16[512,256]{1,0:T(8,128)(2,1)}, bf16[512,256]{1,0:T(8,128)(2,1)S(1)}, u32[]{:S(2)}, u32[]{:S(2)}) collective-permute-start(bf16[512,256]{1,0:T(8,128)(2,1)} %get-tuple-element.190), channel_id=1, source_target_pairs={{0,8},{8,16},{16,24},{24,32},{32,40},{40,48},{48,56},{56,64},{64,7... | collective-permute-start | bytes 786440 | tf_op jit(solution)/shard_map/while/body/eval_jaxpr/ppermute | solution.py:16
  201.2 11.8 %collective-permute-done.1 = bf16[512,256]{1,0:T(8,128)(2,1)S(1)} collective-permute-done((bf16[512,256]{1,0:T(8,128)(2,1)}, bf16[512,256]{1,0:T(8,128)(2,1)S(1)}, u32[]{:S(2)}, u32[]{:S(2)}) %collective-permute-start.1) | collective-permute-done | bytes 262176 | tf_op jit(solution)/shard_map/while/body/eval_jaxpr/ppermute | solution.py:16
  213.8 0.8 constant_dynamic-update-slice_fusion.5
  214.6 3.4 collective-permute-done
  219.4 1.9 collective-permute-start.1
  221.3 3.9 %collective-permute-start = (bf16[512,256]{1,0:T(8,128)(2,1)}, bf16[512,256]{1,0:T(8,128)(2,1)S(1)}, u32[]{:S(2)}, u32[]{:S(2)}) collective-permute-start(bf16[512,256]{1,0:T(8,128)(2,1)} %get-tuple-element.190), channel_id=1, source_target_pairs={{0,8},{8,16},{16,24},{24,32},{32,40},{40,48},{48,56},{56,64},{64,7... | collective-permute-start | bytes 786440 | tf_op jit(solution)/shard_map/while/body/eval_jaxpr/ppermute | solution.py:16
  225.3 12.3 %collective-permute-done.1 = bf16[512,256]{1,0:T(8,128)(2,1)S(1)} collective-permute-done((bf16[512,256]{1,0:T(8,128)(2,1)}, bf16[512,256]{1,0:T(8,128)(2,1)S(1)}, u32[]{:S(2)}, u32[]{:S(2)}) %collective-permute-start.1) | collective-permute-done | bytes 262176 | tf_op jit(solution)/shard_map/while/body/eval_jaxpr/ppermute | solution.py:16
  238.5 0.8 constant_dynamic-update-slice_fusion.5
  239.2 3.9 %collective-permute-done = bf16[512,256]{1,0:T(8,128)(2,1)S(1)} collective-permute-done((bf16[512,256]{1,0:T(8,128)(2,1)}, bf16[512,256]{1,0:T(8,128)(2,1)S(1)}, u32[]{:S(2)}, u32[]{:S(2)}) %collective-permute-start) | collective-permute-done | bytes 262176 | tf_op jit(solution)/shard_map/while/body/eval_jaxpr/ppermute | solution.py:16
  244.5 4.1 %fusion.14 = bf16[4096,256]{0,1:T(8,128)(2,1)} fusion(bf16[4096,256]{0,1:T(8,128)(2,1)} %get-tuple-element.124, s32[]{:T(128)S(6)} %select_n.21, bf16[4096,256]{0,1:T(8,128)(2,1)} %copy.44), kind=kLoop, calls=%fused_computation.26 | loop fusion | flops 4194304 | bytes 6291460 | tf_op jit(solution)/shard_map/add | solution.py:83
  248.6 4.4 %fusion.15 = bf16[4096,256]{1,0:T(8,128)(2,1)} fusion(bf16[4096,256]{1,0:T(8,128)(2,1)S(1)} %copy-done.1, s32[]{:T(128)S(6)} %select_n.21, bf16[4096,256]{1,0:T(8,128)(2,1)S(1)} %copy-done.2), kind=kLoop, calls=%fused_computation.27 | loop fusion | flops 4194304 | bytes 6291460 | tf_op jit(solution)/shard_map/add | solution.py:82
  253.1 1.1 fusion.64
  254.4 9.2 %fusion.4 = (f32[2,512]{1,0:T(2,128)S(1)}, f32[4608,512,2]{1,0,2:T(8,128)}) fusion(pred[512,4608]{0,1:T(8,128)(4,1)S(1)} %fusion.11, bf16[512,2,128]{0,2,1:T(8,128)(2,1)S(1)} %bitcast.106, bf16[4096,256]{1,0:T(8,128)(2,1)} %fusion.15, bf16[512,256]{1,0:T(8,128)(2,1)S(1)} %bitcast.100), kind=kOutput, calls=%fused_computation.10 | convolution fusion | flops 1224473600 | bytes 23859200 | tf_op jit(solution)/shard_map/while/body/eval_jaxpr/qgd,kd->gqk/dot_general | solution.py:42
  263.7 19.0 %fusion = (f32[2,512]{1,0:T(2,128)S(1)}, f32[2,512]{1,0:T(2,128)S(1)}, f32[4608,512,2]{1,0,2:T(8,128)}) fusion(f32[4608,512,2]{1,0,2:T(8,128)} %get-tuple-element.146, f32[2,512]{1,0:T(2,128)S(1)} %get-tuple-element.145, pred[512,4608]{0,1:T(8,128)(4,1)S(1)} %fusion.11, bf16[512,2,128]{0,2,1:T(8,128)(2,1)S(1)} %bitcast.105, ...), kind=kOutput, calls=%fused_computation.6 | convolution fusion | flops 1243346944 | bytes 42741760 | tf_op jit(solution)/shard_map/while/body/eval_jaxpr/qgd,kd->gqk/dot_general | solution.py:42
  282.7 9.8 %fusion.51 = bf16[512,2,128]{0,2,1:T(8,128)(2,1)S(1)} fusion(f32[4608,512,2]{1,0,2:T(8,128)} %get-tuple-element.146, f32[2,512]{1,0:T(2,128)S(1)} %get-tuple-element.145, pred[512,4608]{0,1:T(8,128)(4,1)S(1)} %fusion.11, bf16[4096,256]{0,1:T(8,128)(2,1)S(1)} %copy-done.3, bf16[512,256]{0,1:T(8,128)(2,1)S(1)} %copy-done.6, f32[512,2]{0,1:T(2,128)S(1)} %bitcast.108), kind=kOutput, calls=%fused_computation.45 | convolution fusion | flops 1229455360 | bytes 23863296 | tf_op jit(solution)/shard_map/while/body/eval_jaxpr/gqk,kd->qgd/dot_general | solution.py:50
  292.9 9.9 %fusion.2 = f32[2,512]{1,0:T(2,128)S(1)} fusion(f32[4608,512,2]{1,0,2:T(8,128)} %get-tuple-element.147, f32[2,512]{1,0:T(2,128)S(1)} %get-tuple-element.132, pred[512,4608]{0,1:T(8,128)(4,1)S(1)} %fusion.11), kind=kLoop, calls=%fused_computation.8 | loop fusion | flops 18873344 | bytes 21241856 | tf_op jit(solution)/shard_map/while/body/eval_jaxpr/reduce_sum | solution.py:48
  302.7 1.9 copy-done
  304.7 6.9 %fusion.41 = bf16[512,2,128]{0,2,1:T(8,128)(2,1)S(1)} fusion(f32[4608,512,2]{1,0,2:T(8,128)S(1)} %copy-done, f32[2,512]{1,0:T(2,128)S(1)} %get-tuple-element.132, pred[512,4608]{0,1:T(8,128)(4,1)S(1)} %fusion.11, bf16[512,256]{0,1:T(8,128)(2,1)S(1)} %copy-done.6, bf16[4096,256]{0,1:T(8,128)(2,1)} %fusion.14, f32[512,2]{0,1:T(2,128)S(1)} %bitcast.107), kind=kOutput, calls=%fused_computation.43 | convolution fusion | flops 1229455360 | bytes 23863296 | tf_op jit(solution)/shard_map/while/body/eval_jaxpr/gqk,kd->qgd/dot_general | solution.py:50
  312.0 69.0 %all_to_all.73 = bf16[8,64,512]{2,1,0:T(8,128)(2,1)S(1)} all-to-all(bf16[8,64,512]{2,1,0:T(8,128)(2,1)S(1)} %pad_maximum_fusion.2), channel_id=1, replica_groups=mesh['seq'=32,'head'=8] {'head'}, dimensions={0} | all-to-all | bytes 1048576 | tf_op jit(solution)/shard_map/all_to_all | solution.py:100
  381.0 0.8 copy.68
  (58 shorter events, 19.9 us)
Async XLA Ops:
  0.0 24.8 %copy-start.5 = (bf16[64,4096]{1,0:T(8,128)(2,1)S(1)}, bf16[64,4096]{1,0:T(8,128)(2,1)}, u32[]{:S(2)}) copy-start(bf16[64,4096]{1,0:T(8,128)(2,1)} %param.8) | copy-start | bytes 1572868
  1.7 15.8 %all-to-all-start.1 = ((bf16[64,8,256]{2,0,1:T(8,128)(2,1)}), bf16[64,8,256]{2,0,1:T(8,128)(2,1)}, u32[]{:S(2)}, u32[]{:S(2)}) async-start(bf16[64,8,256]{2,0,1:T(8,128)(2,1)} %bitcast.95), calls=%async_computation.1 | async-start | bytes 524288 | tf_op jit(solution)/shard_map/all_to_all | solution.py:61
  17.5 14.1 %all-to-all-start = ((bf16[64,8,256]{2,0,1:T(8,128)(2,1)}), bf16[64,8,256]{2,0,1:T(8,128)(2,1)S(1)}, u32[]{:S(2)}, u32[]{:S(2)}) async-start(bf16[64,8,256]{2,0,1:T(8,128)(2,1)} %bitcast.96), calls=%async_computation | async-start | bytes 524288 | tf_op jit(solution)/shard_map/all_to_all | solution.py:60
  31.5 221.5 %all-to-all-start.2 = ((bf16[64,8,512]{2,0,1:T(8,128)(2,1)}), bf16[64,8,512]{2,0,1:T(8,128)(2,1)}, u32[]{:S(2)}, u32[]{:S(2)}) async-start(bf16[64,8,512]{2,0,1:T(8,128)(2,1)} %bitcast.94), calls=%async_computation.2 | async-start | bytes 1048576 | tf_op jit(solution)/shard_map/all_to_all | solution.py:59
  40.3 21.0 %collective-permute-start.1 = (bf16[512,256]{1,0:T(8,128)(2,1)}, bf16[512,256]{1,0:T(8,128)(2,1)S(1)}, u32[]{:S(2)}, u32[]{:S(2)}) collective-permute-start(bf16[512,256]{1,0:T(8,128)(2,1)} %get-tuple-element.191), channel_id=1, source_target_pairs={{0,8},{8,16},{16,24},{24,32},{32,40},{40,48},{48,56},{56,64},{64,7... | collective-permute-start | bytes 786440 | tf_op jit(solution)/shard_map/while/body/eval_jaxpr/ppermute | solution.py:16
  47.4 22.2 %collective-permute-start = (bf16[512,256]{1,0:T(8,128)(2,1)}, bf16[512,256]{1,0:T(8,128)(2,1)S(1)}, u32[]{:S(2)}, u32[]{:S(2)}) collective-permute-start(bf16[512,256]{1,0:T(8,128)(2,1)} %get-tuple-element.190), channel_id=1, source_target_pairs={{0,8},{8,16},{16,24},{24,32},{32,40},{40,48},{48,56},{56,64},{64,7... | collective-permute-start | bytes 786440 | tf_op jit(solution)/shard_map/while/body/eval_jaxpr/ppermute | solution.py:16
  71.0 18.2 %collective-permute-start.1 = (bf16[512,256]{1,0:T(8,128)(2,1)}, bf16[512,256]{1,0:T(8,128)(2,1)S(1)}, u32[]{:S(2)}, u32[]{:S(2)}) collective-permute-start(bf16[512,256]{1,0:T(8,128)(2,1)} %get-tuple-element.191), channel_id=1, source_target_pairs={{0,8},{8,16},{16,24},{24,32},{32,40},{40,48},{48,56},{56,64},{64,7... | collective-permute-start | bytes 786440 | tf_op jit(solution)/shard_map/while/body/eval_jaxpr/ppermute | solution.py:16
  73.6 20.4 %collective-permute-start = (bf16[512,256]{1,0:T(8,128)(2,1)}, bf16[512,256]{1,0:T(8,128)(2,1)S(1)}, u32[]{:S(2)}, u32[]{:S(2)}) collective-permute-start(bf16[512,256]{1,0:T(8,128)(2,1)} %get-tuple-element.190), channel_id=1, source_target_pairs={{0,8},{8,16},{16,24},{24,32},{32,40},{40,48},{48,56},{56,64},{64,7... | collective-permute-start | bytes 786440 | tf_op jit(solution)/shard_map/while/body/eval_jaxpr/ppermute | solution.py:16
  95.5 18.3 %collective-permute-start.1 = (bf16[512,256]{1,0:T(8,128)(2,1)}, bf16[512,256]{1,0:T(8,128)(2,1)S(1)}, u32[]{:S(2)}, u32[]{:S(2)}) collective-permute-start(bf16[512,256]{1,0:T(8,128)(2,1)} %get-tuple-element.191), channel_id=1, source_target_pairs={{0,8},{8,16},{16,24},{24,32},{32,40},{40,48},{48,56},{56,64},{64,7... | collective-permute-start | bytes 786440 | tf_op jit(solution)/shard_map/while/body/eval_jaxpr/ppermute | solution.py:16
  97.4 20.2 %collective-permute-start = (bf16[512,256]{1,0:T(8,128)(2,1)}, bf16[512,256]{1,0:T(8,128)(2,1)S(1)}, u32[]{:S(2)}, u32[]{:S(2)}) collective-permute-start(bf16[512,256]{1,0:T(8,128)(2,1)} %get-tuple-element.190), channel_id=1, source_target_pairs={{0,8},{8,16},{16,24},{24,32},{32,40},{40,48},{48,56},{56,64},{64,7... | collective-permute-start | bytes 786440 | tf_op jit(solution)/shard_map/while/body/eval_jaxpr/ppermute | solution.py:16
  119.0 19.0 %collective-permute-start.1 = (bf16[512,256]{1,0:T(8,128)(2,1)}, bf16[512,256]{1,0:T(8,128)(2,1)S(1)}, u32[]{:S(2)}, u32[]{:S(2)}) collective-permute-start(bf16[512,256]{1,0:T(8,128)(2,1)} %get-tuple-element.191), channel_id=1, source_target_pairs={{0,8},{8,16},{16,24},{24,32},{32,40},{40,48},{48,56},{56,64},{64,7... | collective-permute-start | bytes 786440 | tf_op jit(solution)/shard_map/while/body/eval_jaxpr/ppermute | solution.py:16
  120.9 22.7 %collective-permute-start = (bf16[512,256]{1,0:T(8,128)(2,1)}, bf16[512,256]{1,0:T(8,128)(2,1)S(1)}, u32[]{:S(2)}, u32[]{:S(2)}) collective-permute-start(bf16[512,256]{1,0:T(8,128)(2,1)} %get-tuple-element.190), channel_id=1, source_target_pairs={{0,8},{8,16},{16,24},{24,32},{32,40},{40,48},{48,56},{56,64},{64,7... | collective-permute-start | bytes 786440 | tf_op jit(solution)/shard_map/while/body/eval_jaxpr/ppermute | solution.py:16
  145.1 18.2 %collective-permute-start.1 = (bf16[512,256]{1,0:T(8,128)(2,1)}, bf16[512,256]{1,0:T(8,128)(2,1)S(1)}, u32[]{:S(2)}, u32[]{:S(2)}) collective-permute-start(bf16[512,256]{1,0:T(8,128)(2,1)} %get-tuple-element.191), channel_id=1, source_target_pairs={{0,8},{8,16},{16,24},{24,32},{32,40},{40,48},{48,56},{56,64},{64,7... | collective-permute-start | bytes 786440 | tf_op jit(solution)/shard_map/while/body/eval_jaxpr/ppermute | solution.py:16
  147.0 21.1 %collective-permute-start = (bf16[512,256]{1,0:T(8,128)(2,1)}, bf16[512,256]{1,0:T(8,128)(2,1)S(1)}, u32[]{:S(2)}, u32[]{:S(2)}) collective-permute-start(bf16[512,256]{1,0:T(8,128)(2,1)} %get-tuple-element.190), channel_id=1, source_target_pairs={{0,8},{8,16},{16,24},{24,32},{32,40},{40,48},{48,56},{56,64},{64,7... | collective-permute-start | bytes 786440 | tf_op jit(solution)/shard_map/while/body/eval_jaxpr/ppermute | solution.py:16
  169.5 18.3 %collective-permute-start.1 = (bf16[512,256]{1,0:T(8,128)(2,1)}, bf16[512,256]{1,0:T(8,128)(2,1)S(1)}, u32[]{:S(2)}, u32[]{:S(2)}) collective-permute-start(bf16[512,256]{1,0:T(8,128)(2,1)} %get-tuple-element.191), channel_id=1, source_target_pairs={{0,8},{8,16},{16,24},{24,32},{32,40},{40,48},{48,56},{56,64},{64,7... | collective-permute-start | bytes 786440 | tf_op jit(solution)/shard_map/while/body/eval_jaxpr/ppermute | solution.py:16
  171.4 22.0 %collective-permute-start = (bf16[512,256]{1,0:T(8,128)(2,1)}, bf16[512,256]{1,0:T(8,128)(2,1)S(1)}, u32[]{:S(2)}, u32[]{:S(2)}) collective-permute-start(bf16[512,256]{1,0:T(8,128)(2,1)} %get-tuple-element.190), channel_id=1, source_target_pairs={{0,8},{8,16},{16,24},{24,32},{32,40},{40,48},{48,56},{56,64},{64,7... | collective-permute-start | bytes 786440 | tf_op jit(solution)/shard_map/while/body/eval_jaxpr/ppermute | solution.py:16
  194.8 18.2 %collective-permute-start.1 = (bf16[512,256]{1,0:T(8,128)(2,1)}, bf16[512,256]{1,0:T(8,128)(2,1)S(1)}, u32[]{:S(2)}, u32[]{:S(2)}) collective-permute-start(bf16[512,256]{1,0:T(8,128)(2,1)} %get-tuple-element.191), channel_id=1, source_target_pairs={{0,8},{8,16},{16,24},{24,32},{32,40},{40,48},{48,56},{56,64},{64,7... | collective-permute-start | bytes 786440 | tf_op jit(solution)/shard_map/while/body/eval_jaxpr/ppermute | solution.py:16
  196.7 21.3 %collective-permute-start = (bf16[512,256]{1,0:T(8,128)(2,1)}, bf16[512,256]{1,0:T(8,128)(2,1)S(1)}, u32[]{:S(2)}, u32[]{:S(2)}) collective-permute-start(bf16[512,256]{1,0:T(8,128)(2,1)} %get-tuple-element.190), channel_id=1, source_target_pairs={{0,8},{8,16},{16,24},{24,32},{32,40},{40,48},{48,56},{56,64},{64,7... | collective-permute-start | bytes 786440 | tf_op jit(solution)/shard_map/while/body/eval_jaxpr/ppermute | solution.py:16
  219.4 18.2 %collective-permute-start.1 = (bf16[512,256]{1,0:T(8,128)(2,1)}, bf16[512,256]{1,0:T(8,128)(2,1)S(1)}, u32[]{:S(2)}, u32[]{:S(2)}) collective-permute-start(bf16[512,256]{1,0:T(8,128)(2,1)} %get-tuple-element.191), channel_id=1, source_target_pairs={{0,8},{8,16},{16,24},{24,32},{32,40},{40,48},{48,56},{56,64},{64,7... | collective-permute-start | bytes 786440 | tf_op jit(solution)/shard_map/while/body/eval_jaxpr/ppermute | solution.py:16
  221.3 21.8 %collective-permute-start = (bf16[512,256]{1,0:T(8,128)(2,1)}, bf16[512,256]{1,0:T(8,128)(2,1)S(1)}, u32[]{:S(2)}, u32[]{:S(2)}) collective-permute-start(bf16[512,256]{1,0:T(8,128)(2,1)} %get-tuple-element.190), channel_id=1, source_target_pairs={{0,8},{8,16},{16,24},{24,32},{32,40},{40,48},{48,56},{56,64},{64,7... | collective-permute-start | bytes 786440 | tf_op jit(solution)/shard_map/while/body/eval_jaxpr/ppermute | solution.py:16
  244.5 4.1 %copy-start.1 = (bf16[4096,256]{1,0:T(8,128)(2,1)S(1)}, bf16[4096,256]{1,0:T(8,128)(2,1)}, u32[]{:S(2)}) copy-start(bf16[4096,256]{1,0:T(8,128)(2,1)} %get-tuple-element.125) | copy-start | bytes 6291460
  244.5 4.1 %copy-start.2 = (bf16[4096,256]{1,0:T(8,128)(2,1)S(1)}, bf16[4096,256]{1,0:T(8,128)(2,1)}, u32[]{:S(2)}) copy-start(bf16[4096,256]{1,0:T(8,128)(2,1)} %param.11) | copy-start | bytes 6291460
  254.4 9.3 %copy-start.4 = (bf16[4096,256]{1,0:T(8,128)(2,1)S(1)}, bf16[4096,256]{1,0:T(8,128)(2,1)}, u32[]{:S(2)}) copy-start(bf16[4096,256]{1,0:T(8,128)(2,1)} %fusion.15) | copy-start | bytes 6291460
  263.7 19.0 %copy-start.3 = (bf16[4096,256]{0,1:T(8,128)(2,1)S(1)}, bf16[4096,256]{0,1:T(8,128)(2,1)}, u32[]{:S(2)}) copy-start(bf16[4096,256]{0,1:T(8,128)(2,1)} %fusion.14) | copy-start | bytes 6291460
  263.7 19.0 %copy-start.6 = (bf16[512,256]{0,1:T(8,128)(2,1)S(1)}, bf16[512,256]{0,1:T(8,128)(2,1)}, u32[]{:S(2)}) copy-start(bf16[512,256]{0,1:T(8,128)(2,1)} %copy.46) | copy-start | bytes 786436
  292.9 11.8 %copy-start = (f32[4608,512,2]{1,0,2:T(8,128)S(1)}, f32[4608,512,2]{1,0,2:T(8,128)}, u32[]{:S(2)}) copy-start(f32[4608,512,2]{1,0,2:T(8,128)} %get-tuple-element.147) | copy-start | bytes 56623108
where the time goes:
time: 383 us; the launch traced here: 382 us
  waiting for transfers between devices  130 us (34%)
  starting transfers between devices  71.2 us (19%)
  blocking collectives  69 us (18%)
  matrix products  45 us (12%)
  local copies, waits for them, and re-layouts  42.9 us (11%)
  other arithmetic  22.3 us (6%)
    ppermute x16, waiting for transfers between devices, shifted(): return lax.ppermute(shard, axis, pairs)  123 us
    all_to_all x1, blocking collectives, shards(): lax.all_to_all(shortened(attended), 'head', split_axis=0, concat_axis=1,...  69 us
    ppermute x16, starting transfers between devices, shifted(): return lax.ppermute(shard, axis, pairs)  56.9 us
    dot_general x2, matrix products, attend_block(): jnp.einsum('qgd,kd->gqk', query_head, key_head, preferred_element_type=jn...  28.2 us
    dot_general x2, matrix products, attend_block(): jnp.einsum('gqk,kd->qgd', weights, value_head, preferred_element_type=jnp...  16.8 us
    while x16, local copies, waits for them, and re-layouts  11.3 us
    reduce_sum x1, other arithmetic, attend_block(): totals = jnp.sum(unnormed, axis=2)  9.86 us
  transfers between devices with their start and end apart: 19, of which 17 were waited for; matrix products, arithmetic and copies ran while one was open for 13% of the time, Pallas kernels for 0%

commit v1 on v0

--- a/solution.py
+++ b/solution.py
@@ -58,7 +58,12 @@
     query_local, key_local, value_local = (
         lax.all_to_all(queries, "head", split_axis=1, concat_axis=0, tiled=True),
         lax.all_to_all(keys, "head", split_axis=1, concat_axis=0, tiled=True),
-        lax.all_to_all(values, "head", split_axis=1, concat_axis=0, tiled=True),
+        jnp.concatenate(
+            lax.all_to_all(
+                jnp.stack(jnp.split(values, lax.axis_size("head"), axis=1)), "head", 0, 0
+            ),
+            axis=0,
+        ),
     )
     seq_rows = query_local.shape[0]
     shards_back = WINDOW // seq_rows

time: 383 us -> 393 us (1.026)
  local copies, waits for them, and re-layouts: 42.9 us -> 52.3 us
    unnamed x16 -> x23, local copies, waits for them, and re-layouts: 6.78 us -> 16.5 us
  transfers between devices with their start and end apart: 19 -> 19, of which waited for: 17 -> 17; matrix products, arithmetic and copies ran while one was open for 13% -> 12% of each run, Pallas kernels for 0% -> 0%
where the time goes in v1:
time: 393 us; the launch traced here: 391 us
  waiting for transfers between devices  130 us (33%)
  starting transfers between devices  71.2 us (18%)
  blocking collectives  69 us (18%)
  local copies, waits for them, and re-layouts  52.3 us (13%)
  matrix products  45 us (11%)
  other arithmetic  22.3 us (6%)
    ppermute x16, waiting for transfers between devices, shifted(): return lax.ppermute(shard, axis, pairs)  123 us
    all_to_all x1, blocking collectives, shards(): lax.all_to_all(shortened(attended), 'head', split_axis=0, concat_axis=1,...  69 us
    ppermute x16, starting transfers between devices, shifted(): return lax.ppermute(shard, axis, pairs)  56.9 us
    dot_general x2, matrix products, attend_block(): jnp.einsum('qgd,kd->gqk', query_head, key_head, preferred_element_type=jn...  28.2 us
    dot_general x2, matrix products, attend_block(): jnp.einsum('gqk,kd->qgd', weights, value_head, preferred_element_type=jnp...  16.8 us
    unnamed x23, local copies, waits for them, and re-layouts  16.5 us
    while x16, local copies, waits for them, and re-layouts  11.3 us
    reduce_sum x1, other arithmetic, attend_block(): totals = jnp.sum(unnormed, axis=2)  9.86 us
  transfers between devices with their start and end apart: 19, of which 17 were waited for; matrix products, arithmetic and copies ran while one was open for 12% of the time, Pallas kernels for 0%

profile of v1, /device:TPU:16, one launch (start us, length us, event | category | flops | bytes accessed | tf_op | source)
XLA Modules:
  0.0 391.2 jit_solution(9928690206103628419)
XLA Ops:
  0.0 1.4 bitcast_dynamic-update-slice_fusion.7
  1.4 1.4 bitcast_dynamic-update-slice_fusion.6
  2.8 1.4 bitcast_dynamic-update-slice_fusion.5
  4.2 1.4 bitcast_dynamic-update-slice_fusion.4
  5.6 1.4 bitcast_dynamic-update-slice_fusion.3
  6.9 1.4 bitcast_dynamic-update-slice_fusion.2
  8.3 1.4 bitcast_dynamic-update-slice_fusion.1
  9.7 1.4 bitcast_dynamic-update-slice_fusion
  11.1 5.9 %all-to-all-start.1 = ((bf16[8,64,256]{2,1,0:T(8,128)(2,1)}), bf16[8,64,256]{2,1,0:T(8,128)(2,1)}, u32[]{:S(2)}, u32[]{:S(2)}) async-start(bf16[8,64,256]{2,1,0:T(8,128)(2,1)} %bitcast_dynamic-update-slice_fusion), calls=%async_computation.1 | async-start | bytes 524288 | tf_op jit(solution)/shard_map/all_to_all | solution.py:62
  17.6 1.7 copy.69
  19.3 7.5 %all-to-all-done.1 = bf16[8,64,256]{2,1,0:T(8,128)(2,1)} async-done(((bf16[8,64,256]{2,1,0:T(8,128)(2,1)}), bf16[8,64,256]{2,1,0:T(8,128)(2,1)}, u32[]{:S(2)}, u32[]{:S(2)}) %all-to-all-start.1) | async-done | bytes 262176 | tf_op jit(solution)/shard_map/all_to_all | solution.py:62
  26.8 3.4 all-to-all-start
  30.2 3.8 fusion.11
  34.1 0.8 copy.68
  34.9 4.1 %copy.42 = bf16[4096,256]{0,1:T(8,128)(2,1)} copy(bf16[4096,256]{1,0:T(8,128)(2,1)} %param.12) | data formatting | bytes 4194304 | tf_op args[4]
  39.1 1.8 copy.44
  40.9 5.0 %all-to-all-start.2 = ((bf16[64,8,512]{2,0,1:T(8,128)(2,1)}), bf16[64,8,512]{2,0,1:T(8,128)(2,1)}, u32[]{:S(2)}, u32[]{:S(2)}) async-start(bf16[64,8,512]{2,0,1:T(8,128)(2,1)} %bitcast.105), calls=%async_computation.2 | async-start | bytes 1048576 | tf_op jit(solution)/shard_map/all_to_all | solution.py:59
  46.6 1.6 broadcast.86.clone
  48.2 1.4 broadcast.86
  49.6 204.3 %while.6 = (s32[]{:T(128)}, bf16[512,256]{1,0:T(8,128)(2,1)}, bf16[512,256]{1,0:T(8,128)(2,1)}, bf16[4096,256]{1,0:T(8,128)(2,1)}, bf16[4096,256]{0,1:T(8,128)(2...) while((s32[]{:T(128)}, bf16[512,256]{1,0:T(8,128)(2,1)}, bf16[512,256]{1,0:T(8,128)(2,1)}, ...), condition=%wide.region_1.0_spmd, body=%wide.region_0.0_spmd.sunk | while | flops 7 | bytes 4718839 | solution.py:81
  49.6 7.1 %collective-permute-start.1 = (bf16[512,256]{1,0:T(8,128)(2,1)}, bf16[512,256]{1,0:T(8,128)(2,1)S(1)}, u32[]{:S(2)}, u32[]{:S(2)}) collective-permute-start(bf16[512,256]{1,0:T(8,128)(2,1)} %get-tuple-element.191), channel_id=1, source_target_pairs={{0,8},{8,16},{16,24},{24,32},{32,40},{40,48},{48,56},{56,64},{64,7... | collective-permute-start | bytes 786440 | tf_op jit(solution)/shard_map/while/body/eval_jaxpr/ppermute | solution.py:16
  56.7 3.5 collective-permute-start
  60.3 10.3 %collective-permute-done.1 = bf16[512,256]{1,0:T(8,128)(2,1)S(1)} collective-permute-done((bf16[512,256]{1,0:T(8,128)(2,1)}, bf16[512,256]{1,0:T(8,128)(2,1)S(1)}, u32[]{:S(2)}, u32[]{:S(2)}) %collective-permute-start.1) | collective-permute-done | bytes 262176 | tf_op jit(solution)/shard_map/while/body/eval_jaxpr/ppermute | solution.py:16
  72.2 6.7 %collective-permute-done = bf16[512,256]{1,0:T(8,128)(2,1)S(1)} collective-permute-done((bf16[512,256]{1,0:T(8,128)(2,1)}, bf16[512,256]{1,0:T(8,128)(2,1)S(1)}, u32[]{:S(2)}, u32[]{:S(2)}) %collective-permute-start) | collective-permute-done | bytes 262176 | tf_op jit(solution)/shard_map/while/body/eval_jaxpr/ppermute | solution.py:16
  80.3 2.6 collective-permute-start.1
  82.9 5.9 %collective-permute-start = (bf16[512,256]{1,0:T(8,128)(2,1)}, bf16[512,256]{1,0:T(8,128)(2,1)S(1)}, u32[]{:S(2)}, u32[]{:S(2)}) collective-permute-start(bf16[512,256]{1,0:T(8,128)(2,1)} %get-tuple-element.190), channel_id=1, source_target_pairs={{0,8},{8,16},{16,24},{24,32},{32,40},{40,48},{48,56},{56,64},{64,7... | collective-permute-start | bytes 786440 | tf_op jit(solution)/shard_map/while/body/eval_jaxpr/ppermute | solution.py:16
  88.9 9.6 %collective-permute-done.1 = bf16[512,256]{1,0:T(8,128)(2,1)S(1)} collective-permute-done((bf16[512,256]{1,0:T(8,128)(2,1)}, bf16[512,256]{1,0:T(8,128)(2,1)S(1)}, u32[]{:S(2)}, u32[]{:S(2)}) %collective-permute-start.1) | collective-permute-done | bytes 262176 | tf_op jit(solution)/shard_map/while/body/eval_jaxpr/ppermute | solution.py:16
  99.4 0.8 constant_dynamic-update-slice_fusion.5
  100.1 3.2 collective-permute-done
  104.8 1.9 collective-permute-start.1
  106.7 4.3 %collective-permute-start = (bf16[512,256]{1,0:T(8,128)(2,1)}, bf16[512,256]{1,0:T(8,128)(2,1)S(1)}, u32[]{:S(2)}, u32[]{:S(2)}) collective-permute-start(bf16[512,256]{1,0:T(8,128)(2,1)} %get-tuple-element.190), channel_id=1, source_target_pairs={{0,8},{8,16},{16,24},{24,32},{32,40},{40,48},{48,56},{56,64},{64,7... | collective-permute-start | bytes 786440 | tf_op jit(solution)/shard_map/while/body/eval_jaxpr/ppermute | solution.py:16
  111.1 12.0 %collective-permute-done.1 = bf16[512,256]{1,0:T(8,128)(2,1)S(1)} collective-permute-done((bf16[512,256]{1,0:T(8,128)(2,1)}, bf16[512,256]{1,0:T(8,128)(2,1)S(1)}, u32[]{:S(2)}, u32[]{:S(2)}) %collective-permute-start.1) | collective-permute-done | bytes 262176 | tf_op jit(solution)/shard_map/while/body/eval_jaxpr/ppermute | solution.py:16
  124.7 2.3 collective-permute-done
  128.3 1.9 collective-permute-start.1
  130.3 4.8 %collective-permute-start = (bf16[512,256]{1,0:T(8,128)(2,1)}, bf16[512,256]{1,0:T(8,128)(2,1)S(1)}, u32[]{:S(2)}, u32[]{:S(2)}) collective-permute-start(bf16[512,256]{1,0:T(8,128)(2,1)} %get-tuple-element.190), channel_id=1, source_target_pairs={{0,8},{8,16},{16,24},{24,32},{32,40},{40,48},{48,56},{56,64},{64,7... | collective-permute-start | bytes 786440 | tf_op jit(solution)/shard_map/while/body/eval_jaxpr/ppermute | solution.py:16
  135.1 12.2 %collective-permute-done.1 = bf16[512,256]{1,0:T(8,128)(2,1)S(1)} collective-permute-done((bf16[512,256]{1,0:T(8,128)(2,1)}, bf16[512,256]{1,0:T(8,128)(2,1)S(1)}, u32[]{:S(2)}, u32[]{:S(2)}) %collective-permute-start.1) | collective-permute-done | bytes 262176 | tf_op jit(solution)/shard_map/while/body/eval_jaxpr/ppermute | solution.py:16
  148.9 4.0 %collective-permute-done = bf16[512,256]{1,0:T(8,128)(2,1)S(1)} collective-permute-done((bf16[512,256]{1,0:T(8,128)(2,1)}, bf16[512,256]{1,0:T(8,128)(2,1)S(1)}, u32[]{:S(2)}, u32[]{:S(2)}) %collective-permute-start) | collective-permute-done | bytes 262176 | tf_op jit(solution)/shard_map/while/body/eval_jaxpr/ppermute | solution.py:16
  154.4 1.9 collective-permute-start.1
  156.3 4.5 %collective-permute-start = (bf16[512,256]{1,0:T(8,128)(2,1)}, bf16[512,256]{1,0:T(8,128)(2,1)S(1)}, u32[]{:S(2)}, u32[]{:S(2)}) collective-permute-start(bf16[512,256]{1,0:T(8,128)(2,1)} %get-tuple-element.190), channel_id=1, source_target_pairs={{0,8},{8,16},{16,24},{24,32},{32,40},{40,48},{48,56},{56,64},{64,7... | collective-permute-start | bytes 786440 | tf_op jit(solution)/shard_map/while/body/eval_jaxpr/ppermute | solution.py:16
  160.8 11.7 %collective-permute-done.1 = bf16[512,256]{1,0:T(8,128)(2,1)S(1)} collective-permute-done((bf16[512,256]{1,0:T(8,128)(2,1)}, bf16[512,256]{1,0:T(8,128)(2,1)S(1)}, u32[]{:S(2)}, u32[]{:S(2)}) %collective-permute-start.1) | collective-permute-done | bytes 262176 | tf_op jit(solution)/shard_map/while/body/eval_jaxpr/ppermute | solution.py:16
  174.2 3.2 collective-permute-done
  178.8 1.9 collective-permute-start.1
  180.7 4.1 %collective-permute-start = (bf16[512,256]{1,0:T(8,128)(2,1)}, bf16[512,256]{1,0:T(8,128)(2,1)S(1)}, u32[]{:S(2)}, u32[]{:S(2)}) collective-permute-start(bf16[512,256]{1,0:T(8,128)(2,1)} %get-tuple-element.190), channel_id=1, source_target_pairs={{0,8},{8,16},{16,24},{24,32},{32,40},{40,48},{48,56},{56,64},{64,7... | collective-permute-start | bytes 786440 | tf_op jit(solution)/shard_map/while/body/eval_jaxpr/ppermute | solution.py:16
  184.9 12.2 %collective-permute-done.1 = bf16[512,256]{1,0:T(8,128)(2,1)S(1)} collective-permute-done((bf16[512,256]{1,0:T(8,128)(2,1)}, bf16[512,256]{1,0:T(8,128)(2,1)S(1)}, u32[]{:S(2)}, u32[]{:S(2)}) %collective-permute-start.1) | collective-permute-done | bytes 262176 | tf_op jit(solution)/shard_map/while/body/eval_jaxpr/ppermute | solution.py:16
  198.7 4.0 %collective-permute-done = bf16[512,256]{1,0:T(8,128)(2,1)S(1)} collective-permute-done((bf16[512,256]{1,0:T(8,128)(2,1)}, bf16[512,256]{1,0:T(8,128)(2,1)S(1)}, u32[]{:S(2)}, u32[]{:S(2)}) %collective-permute-start) | collective-permute-done | bytes 262176 | tf_op jit(solution)/shard_map/while/body/eval_jaxpr/ppermute | solution.py:16
  204.1 1.9 collective-permute-start.1
  206.0 4.5 %collective-permute-start = (bf16[512,256]{1,0:T(8,128)(2,1)}, bf16[512,256]{1,0:T(8,128)(2,1)S(1)}, u32[]{:S(2)}, u32[]{:S(2)}) collective-permute-start(bf16[512,256]{1,0:T(8,128)(2,1)} %get-tuple-element.190), channel_id=1, source_target_pairs={{0,8},{8,16},{16,24},{24,32},{32,40},{40,48},{48,56},{56,64},{64,7... | collective-permute-start | bytes 786440 | tf_op jit(solution)/shard_map/while/body/eval_jaxpr/ppermute | solution.py:16
  210.5 11.8 %collective-permute-done.1 = bf16[512,256]{1,0:T(8,128)(2,1)S(1)} collective-permute-done((bf16[512,256]{1,0:T(8,128)(2,1)}, bf16[512,256]{1,0:T(8,128)(2,1)S(1)}, u32[]{:S(2)}, u32[]{:S(2)}) %collective-permute-start.1) | collective-permute-done | bytes 262176 | tf_op jit(solution)/shard_map/while/body/eval_jaxpr/ppermute | solution.py:16
  223.9 3.4 collective-permute-done
  228.7 1.9 collective-permute-start.1
  230.7 3.9 %collective-permute-start = (bf16[512,256]{1,0:T(8,128)(2,1)}, bf16[512,256]{1,0:T(8,128)(2,1)S(1)}, u32[]{:S(2)}, u32[]{:S(2)}) collective-permute-start(bf16[512,256]{1,0:T(8,128)(2,1)} %get-tuple-element.190), channel_id=1, source_target_pairs={{0,8},{8,16},{16,24},{24,32},{32,40},{40,48},{48,56},{56,64},{64,7... | collective-permute-start | bytes 786440 | tf_op jit(solution)/shard_map/while/body/eval_jaxpr/ppermute | solution.py:16
  234.6 12.3 %collective-permute-done.1 = bf16[512,256]{1,0:T(8,128)(2,1)S(1)} collective-permute-done((bf16[512,256]{1,0:T(8,128)(2,1)}, bf16[512,256]{1,0:T(8,128)(2,1)S(1)}, u32[]{:S(2)}, u32[]{:S(2)}) %collective-permute-start.1) | collective-permute-done | bytes 262176 | tf_op jit(solution)/shard_map/while/body/eval_jaxpr/ppermute | solution.py:16
  248.5 3.9 %collective-permute-done = bf16[512,256]{1,0:T(8,128)(2,1)S(1)} collective-permute-done((bf16[512,256]{1,0:T(8,128)(2,1)}, bf16[512,256]{1,0:T(8,128)(2,1)S(1)}, u32[]{:S(2)}, u32[]{:S(2)}) %collective-permute-start) | collective-permute-done | bytes 262176 | tf_op jit(solution)/shard_map/while/body/eval_jaxpr/ppermute | solution.py:16
  253.9 4.1 %fusion.14 = bf16[4096,256]{0,1:T(8,128)(2,1)} fusion(bf16[4096,256]{0,1:T(8,128)(2,1)} %get-tuple-element.124, s32[]{:T(128)S(6)} %select_n.21, bf16[4096,256]{0,1:T(8,128)(2,1)} %copy.42), kind=kLoop, calls=%fused_computation.26 | loop fusion | flops 4194304 | bytes 6291460 | tf_op jit(solution)/shard_map/add | solution.py:88
  258.0 4.4 %fusion.15 = bf16[4096,256]{1,0:T(8,128)(2,1)} fusion(bf16[4096,256]{1,0:T(8,128)(2,1)S(1)} %copy-done.1, s32[]{:T(128)S(6)} %select_n.21, bf16[4096,256]{1,0:T(8,128)(2,1)S(1)} %copy-done.2), kind=kLoop, calls=%fused_computation.27 | loop fusion | flops 4194304 | bytes 6291460 | tf_op jit(solution)/shard_map/add | solution.py:87
  262.4 1.1 fusion.64
  263.8 9.2 %fusion.4 = (f32[2,512]{1,0:T(2,128)S(1)}, f32[4608,512,2]{1,0,2:T(8,128)}) fusion(pred[512,4608]{0,1:T(8,128)(4,1)S(1)} %fusion.11, bf16[512,2,128]{0,2,1:T(8,128)(2,1)S(1)} %bitcast.115, bf16[4096,256]{1,0:T(8,128)(2,1)} %fusion.15, bf16[512,256]{1,0:T(8,128)(2,1)S(1)} %bitcast.110), kind=kOutput, calls=%fused_computation.10 | convolution fusion | flops 1224473600 | bytes 23859200 | tf_op jit(solution)/shard_map/while/body/eval_jaxpr/qgd,kd->gqk/dot_general | solution.py:42
  273.0 19.0 %fusion = (f32[2,512]{1,0:T(2,128)S(1)}, f32[2,512]{1,0:T(2,128)S(1)}, f32[4608,512,2]{1,0,2:T(8,128)}) fusion(f32[4608,512,2]{1,0,2:T(8,128)} %get-tuple-element.146, f32[2,512]{1,0:T(2,128)S(1)} %get-tuple-element.145, pred[512,4608]{0,1:T(8,128)(4,1)S(1)} %fusion.11, bf16[512,2,128]{0,2,1:T(8,128)(2,1)S(1)} %bitcast.114, ...), kind=kOutput, calls=%fused_computation.6 | convolution fusion | flops 1243346944 | bytes 42741760 | tf_op jit(solution)/shard_map/while/body/eval_jaxpr/qgd,kd->gqk/dot_general | solution.py:42
  292.0 9.8 %fusion.51 = bf16[512,2,128]{0,2,1:T(8,128)(2,1)S(1)} fusion(f32[4608,512,2]{1,0,2:T(8,128)} %get-tuple-element.146, f32[2,512]{1,0:T(2,128)S(1)} %get-tuple-element.145, pred[512,4608]{0,1:T(8,128)(4,1)S(1)} %fusion.11, bf16[4096,256]{0,1:T(8,128)(2,1)S(1)} %copy-done.3, bf16[512,256]{0,1:T(8,128)(2,1)S(1)} %copy-done.6, f32[512,2]{0,1:T(2,128)S(1)} %bitcast.117), kind=kOutput, calls=%fused_computation.45 | convolution fusion | flops 1229455360 | bytes 23863296 | tf_op jit(solution)/shard_map/while/body/eval_jaxpr/gqk,kd->qgd/dot_general | solution.py:50
  302.2 9.9 %fusion.2 = f32[2,512]{1,0:T(2,128)S(1)} fusion(f32[4608,512,2]{1,0,2:T(8,128)} %get-tuple-element.147, f32[2,512]{1,0:T(2,128)S(1)} %get-tuple-element.132, pred[512,4608]{0,1:T(8,128)(4,1)S(1)} %fusion.11), kind=kLoop, calls=%fused_computation.8 | loop fusion | flops 18873344 | bytes 21241856 | tf_op jit(solution)/shard_map/while/body/eval_jaxpr/reduce_sum | solution.py:48
  312.1 1.9 copy-done
  314.0 6.9 %fusion.41 = bf16[512,2,128]{0,2,1:T(8,128)(2,1)S(1)} fusion(f32[4608,512,2]{1,0,2:T(8,128)S(1)} %copy-done, f32[2,512]{1,0:T(2,128)S(1)} %get-tuple-element.132, pred[512,4608]{0,1:T(8,128)(4,1)S(1)} %fusion.11, bf16[512,256]{0,1:T(8,128)(2,1)S(1)} %copy-done.6, bf16[4096,256]{0,1:T(8,128)(2,1)} %fusion.14, f32[512,2]{0,1:T(2,128)S(1)} %bitcast.116), kind=kOutput, calls=%fused_computation.43 | convolution fusion | flops 1229455360 | bytes 23863296 | tf_op jit(solution)/shard_map/while/body/eval_jaxpr/gqk,kd->qgd/dot_general | solution.py:50
  321.3 69.0 %all_to_all.59 = bf16[8,64,512]{2,1,0:T(8,128)(2,1)S(1)} all-to-all(bf16[8,64,512]{2,1,0:T(8,128)(2,1)S(1)} %pad_maximum_fusion.2), channel_id=1, replica_groups=mesh['seq'=32,'head'=8] {'head'}, dimensions={0} | all-to-all | bytes 1048576 | tf_op jit(solution)/shard_map/all_to_all | solution.py:105
  390.4 0.8 copy.65
  (65 shorter events, 25.2 us)
Async XLA Ops:
  0.0 34.1 %copy-start.5 = (bf16[64,4096]{1,0:T(8,128)(2,1)S(1)}, bf16[64,4096]{1,0:T(8,128)(2,1)}, u32[]{:S(2)}) copy-start(bf16[64,4096]{1,0:T(8,128)(2,1)} %param.8) | copy-start | bytes 1572868
  11.1 15.8 %all-to-all-start.1 = ((bf16[8,64,256]{2,1,0:T(8,128)(2,1)}), bf16[8,64,256]{2,1,0:T(8,128)(2,1)}, u32[]{:S(2)}, u32[]{:S(2)}) async-start(bf16[8,64,256]{2,1,0:T(8,128)(2,1)} %bitcast_dynamic-update-slice_fusion), calls=%async_computation.1 | async-start | bytes 524288 | tf_op jit(solution)/shard_map/all_to_all | solution.py:62
  26.8 14.1 %all-to-all-start = ((bf16[64,8,256]{2,0,1:T(8,128)(2,1)}), bf16[64,8,256]{2,0,1:T(8,128)(2,1)S(1)}, u32[]{:S(2)}, u32[]{:S(2)}) async-start(bf16[64,8,256]{2,0,1:T(8,128)(2,1)} %bitcast.106), calls=%async_computation | async-start | bytes 524288 | tf_op jit(solution)/shard_map/all_to_all | solution.py:60
  40.9 221.5 %all-to-all-start.2 = ((bf16[64,8,512]{2,0,1:T(8,128)(2,1)}), bf16[64,8,512]{2,0,1:T(8,128)(2,1)}, u32[]{:S(2)}, u32[]{:S(2)}) async-start(bf16[64,8,512]{2,0,1:T(8,128)(2,1)} %bitcast.105), calls=%async_computation.2 | async-start | bytes 1048576 | tf_op jit(solution)/shard_map/all_to_all | solution.py:59
  49.6 21.0 %collective-permute-start.1 = (bf16[512,256]{1,0:T(8,128)(2,1)}, bf16[512,256]{1,0:T(8,128)(2,1)S(1)}, u32[]{:S(2)}, u32[]{:S(2)}) collective-permute-start(bf16[512,256]{1,0:T(8,128)(2,1)} %get-tuple-element.191), channel_id=1, source_target_pairs={{0,8},{8,16},{16,24},{24,32},{32,40},{40,48},{48,56},{56,64},{64,7... | collective-permute-start | bytes 786440 | tf_op jit(solution)/shard_map/while/body/eval_jaxpr/ppermute | solution.py:16
  56.7 22.2 %collective-permute-start = (bf16[512,256]{1,0:T(8,128)(2,1)}, bf16[512,256]{1,0:T(8,128)(2,1)S(1)}, u32[]{:S(2)}, u32[]{:S(2)}) collective-permute-start(bf16[512,256]{1,0:T(8,128)(2,1)} %get-tuple-element.190), channel_id=1, source_target_pairs={{0,8},{8,16},{16,24},{24,32},{32,40},{40,48},{48,56},{56,64},{64,7... | collective-permute-start | bytes 786440 | tf_op jit(solution)/shard_map/while/body/eval_jaxpr/ppermute | solution.py:16
  80.3 18.2 %collective-permute-start.1 = (bf16[512,256]{1,0:T(8,128)(2,1)}, bf16[512,256]{1,0:T(8,128)(2,1)S(1)}, u32[]{:S(2)}, u32[]{:S(2)}) collective-permute-start(bf16[512,256]{1,0:T(8,128)(2,1)} %get-tuple-element.191), channel_id=1, source_target_pairs={{0,8},{8,16},{16,24},{24,32},{32,40},{40,48},{48,56},{56,64},{64,7... | collective-permute-start | bytes 786440 | tf_op jit(solution)/shard_map/while/body/eval_jaxpr/ppermute | solution.py:16
  82.9 20.4 %collective-permute-start = (bf16[512,256]{1,0:T(8,128)(2,1)}, bf16[512,256]{1,0:T(8,128)(2,1)S(1)}, u32[]{:S(2)}, u32[]{:S(2)}) collective-permute-start(bf16[512,256]{1,0:T(8,128)(2,1)} %get-tuple-element.190), channel_id=1, source_target_pairs={{0,8},{8,16},{16,24},{24,32},{32,40},{40,48},{48,56},{56,64},{64,7... | collective-permute-start | bytes 786440 | tf_op jit(solution)/shard_map/while/body/eval_jaxpr/ppermute | solution.py:16
  104.8 18.3 %collective-permute-start.1 = (bf16[512,256]{1,0:T(8,128)(2,1)}, bf16[512,256]{1,0:T(8,128)(2,1)S(1)}, u32[]{:S(2)}, u32[]{:S(2)}) collective-permute-start(bf16[512,256]{1,0:T(8,128)(2,1)} %get-tuple-element.191), channel_id=1, source_target_pairs={{0,8},{8,16},{16,24},{24,32},{32,40},{40,48},{48,56},{56,64},{64,7... | collective-permute-start | bytes 786440 | tf_op jit(solution)/shard_map/while/body/eval_jaxpr/ppermute | solution.py:16
  106.7 20.2 %collective-permute-start = (bf16[512,256]{1,0:T(8,128)(2,1)}, bf16[512,256]{1,0:T(8,128)(2,1)S(1)}, u32[]{:S(2)}, u32[]{:S(2)}) collective-permute-start(bf16[512,256]{1,0:T(8,128)(2,1)} %get-tuple-element.190), channel_id=1, source_target_pairs={{0,8},{8,16},{16,24},{24,32},{32,40},{40,48},{48,56},{56,64},{64,7... | collective-permute-start | bytes 786440 | tf_op jit(solution)/shard_map/while/body/eval_jaxpr/ppermute | solution.py:16
  128.3 19.0 %collective-permute-start.1 = (bf16[512,256]{1,0:T(8,128)(2,1)}, bf16[512,256]{1,0:T(8,128)(2,1)S(1)}, u32[]{:S(2)}, u32[]{:S(2)}) collective-permute-start(bf16[512,256]{1,0:T(8,128)(2,1)} %get-tuple-element.191), channel_id=1, source_target_pairs={{0,8},{8,16},{16,24},{24,32},{32,40},{40,48},{48,56},{56,64},{64,7... | collective-permute-start | bytes 786440 | tf_op jit(solution)/shard_map/while/body/eval_jaxpr/ppermute | solution.py:16
  130.3 22.7 %collective-permute-start = (bf16[512,256]{1,0:T(8,128)(2,1)}, bf16[512,256]{1,0:T(8,128)(2,1)S(1)}, u32[]{:S(2)}, u32[]{:S(2)}) collective-permute-start(bf16[512,256]{1,0:T(8,128)(2,1)} %get-tuple-element.190), channel_id=1, source_target_pairs={{0,8},{8,16},{16,24},{24,32},{32,40},{40,48},{48,56},{56,64},{64,7... | collective-permute-start | bytes 786440 | tf_op jit(solution)/shard_map/while/body/eval_jaxpr/ppermute | solution.py:16
  154.4 18.2 %collective-permute-start.1 = (bf16[512,256]{1,0:T(8,128)(2,1)}, bf16[512,256]{1,0:T(8,128)(2,1)S(1)}, u32[]{:S(2)}, u32[]{:S(2)}) collective-permute-start(bf16[512,256]{1,0:T(8,128)(2,1)} %get-tuple-element.191), channel_id=1, source_target_pairs={{0,8},{8,16},{16,24},{24,32},{32,40},{40,48},{48,56},{56,64},{64,7... | collective-permute-start | bytes 786440 | tf_op jit(solution)/shard_map/while/body/eval_jaxpr/ppermute | solution.py:16
  156.3 21.1 %collective-permute-start = (bf16[512,256]{1,0:T(8,128)(2,1)}, bf16[512,256]{1,0:T(8,128)(2,1)S(1)}, u32[]{:S(2)}, u32[]{:S(2)}) collective-permute-start(bf16[512,256]{1,0:T(8,128)(2,1)} %get-tuple-element.190), channel_id=1, source_target_pairs={{0,8},{8,16},{16,24},{24,32},{32,40},{40,48},{48,56},{56,64},{64,7... | collective-permute-start | bytes 786440 | tf_op jit(solution)/shard_map/while/body/eval_jaxpr/ppermute | solution.py:16
  178.8 18.3 %collective-permute-start.1 = (bf16[512,256]{1,0:T(8,128)(2,1)}, bf16[512,256]{1,0:T(8,128)(2,1)S(1)}, u32[]{:S(2)}, u32[]{:S(2)}) collective-permute-start(bf16[512,256]{1,0:T(8,128)(2,1)} %get-tuple-element.191), channel_id=1, source_target_pairs={{0,8},{8,16},{16,24},{24,32},{32,40},{40,48},{48,56},{56,64},{64,7... | collective-permute-start | bytes 786440 | tf_op jit(solution)/shard_map/while/body/eval_jaxpr/ppermute | solution.py:16
  180.7 22.0 %collective-permute-start = (bf16[512,256]{1,0:T(8,128)(2,1)}, bf16[512,256]{1,0:T(8,128)(2,1)S(1)}, u32[]{:S(2)}, u32[]{:S(2)}) collective-permute-start(bf16[512,256]{1,0:T(8,128)(2,1)} %get-tuple-element.190), channel_id=1, source_target_pairs={{0,8},{8,16},{16,24},{24,32},{32,40},{40,48},{48,56},{56,64},{64,7... | collective-permute-start | bytes 786440 | tf_op jit(solution)/shard_map/while/body/eval_jaxpr/ppermute | solution.py:16
  204.1 18.2 %collective-permute-start.1 = (bf16[512,256]{1,0:T(8,128)(2,1)}, bf16[512,256]{1,0:T(8,128)(2,1)S(1)}, u32[]{:S(2)}, u32[]{:S(2)}) collective-permute-start(bf16[512,256]{1,0:T(8,128)(2,1)} %get-tuple-element.191), channel_id=1, source_target_pairs={{0,8},{8,16},{16,24},{24,32},{32,40},{40,48},{48,56},{56,64},{64,7... | collective-permute-start | bytes 786440 | tf_op jit(solution)/shard_map/while/body/eval_jaxpr/ppermute | solution.py:16
  206.0 21.3 %collective-permute-start = (bf16[512,256]{1,0:T(8,128)(2,1)}, bf16[512,256]{1,0:T(8,128)(2,1)S(1)}, u32[]{:S(2)}, u32[]{:S(2)}) collective-permute-start(bf16[512,256]{1,0:T(8,128)(2,1)} %get-tuple-element.190), channel_id=1, source_target_pairs={{0,8},{8,16},{16,24},{24,32},{32,40},{40,48},{48,56},{56,64},{64,7... | collective-permute-start | bytes 786440 | tf_op jit(solution)/shard_map/while/body/eval_jaxpr/ppermute | solution.py:16
  228.7 18.2 %collective-permute-start.1 = (bf16[512,256]{1,0:T(8,128)(2,1)}, bf16[512,256]{1,0:T(8,128)(2,1)S(1)}, u32[]{:S(2)}, u32[]{:S(2)}) collective-permute-start(bf16[512,256]{1,0:T(8,128)(2,1)} %get-tuple-element.191), channel_id=1, source_target_pairs={{0,8},{8,16},{16,24},{24,32},{32,40},{40,48},{48,56},{56,64},{64,7... | collective-permute-start | bytes 786440 | tf_op jit(solution)/shard_map/while/body/eval_jaxpr/ppermute | solution.py:16
  230.7 21.8 %collective-permute-start = (bf16[512,256]{1,0:T(8,128)(2,1)}, bf16[512,256]{1,0:T(8,128)(2,1)S(1)}, u32[]{:S(2)}, u32[]{:S(2)}) collective-permute-start(bf16[512,256]{1,0:T(8,128)(2,1)} %get-tuple-element.190), channel_id=1, source_target_pairs={{0,8},{8,16},{16,24},{24,32},{32,40},{40,48},{48,56},{56,64},{64,7... | collective-permute-start | bytes 786440 | tf_op jit(solution)/shard_map/while/body/eval_jaxpr/ppermute | solution.py:16
  253.9 4.1 %copy-start.1 = (bf16[4096,256]{1,0:T(8,128)(2,1)S(1)}, bf16[4096,256]{1,0:T(8,128)(2,1)}, u32[]{:S(2)}) copy-start(bf16[4096,256]{1,0:T(8,128)(2,1)} %get-tuple-element.125) | copy-start | bytes 6291460
  253.9 4.1 %copy-start.2 = (bf16[4096,256]{1,0:T(8,128)(2,1)S(1)}, bf16[4096,256]{1,0:T(8,128)(2,1)}, u32[]{:S(2)}) copy-start(bf16[4096,256]{1,0:T(8,128)(2,1)} %param.11) | copy-start | bytes 6291460
  263.8 9.3 %copy-start.4 = (bf16[4096,256]{1,0:T(8,128)(2,1)S(1)}, bf16[4096,256]{1,0:T(8,128)(2,1)}, u32[]{:S(2)}) copy-start(bf16[4096,256]{1,0:T(8,128)(2,1)} %fusion.15) | copy-start | bytes 6291460
  273.0 19.0 %copy-start.3 = (bf16[4096,256]{0,1:T(8,128)(2,1)S(1)}, bf16[4096,256]{0,1:T(8,128)(2,1)}, u32[]{:S(2)}) copy-start(bf16[4096,256]{0,1:T(8,128)(2,1)} %fusion.14) | copy-start | bytes 6291460
  273.0 19.0 %copy-start.6 = (bf16[512,256]{0,1:T(8,128)(2,1)S(1)}, bf16[512,256]{0,1:T(8,128)(2,1)}, u32[]{:S(2)}) copy-start(bf16[512,256]{0,1:T(8,128)(2,1)} %copy.44) | copy-start | bytes 786436
  302.2 11.8 %copy-start = (f32[4608,512,2]{1,0,2:T(8,128)S(1)}, f32[4608,512,2]{1,0,2:T(8,128)}, u32[]{:S(2)}) copy-start(f32[4608,512,2]{1,0,2:T(8,128)} %get-tuple-element.147) | copy-start | bytes 56623108
